TPU v7x, 256 devices: a whole 4x4x8 slice. The times are simulated.
256 devices in a mesh: kx: 8 (over z), ht: 8 (over y, core), real: 4 (over x).
Axes of the slice: x: 4, y: 4, z: 8, core: 2. Of those that a mesh axis runs over, the one named last changes fastest.
Arguments:
- velocity: float32 [3, 4, 32, 512, 128], P(None, 'real', 'kx', 'ht'), may hold values from -6 to 6
- low_index: int32 [8], replicated, may hold values from 0 to 31, as said below
- neighbours: int32 [32, 8], P('kx'), may hold values from 0 to 31, as said below
- owner_map: int32 [64], replicated, may hold values from 0 to 63, each once
- mode_counts: int32 [32], P('kx'), may hold values from 16 to 64
- helmholtz: float32 [64, 512, 512], P(('kx', 'ht')), may hold values from -0.25 to 0.25
Outputs:
- velocity_next: float32 [3, 4, 32, 512, 128], P(None, 'real', 'kx', 'ht')
Inputs may be any that keep to these rules, and one draw needn't show every extreme that they name: `low_index`: distinct values. neighbours[m, j] lies within 4 modes of m, counting circularly over the 32 modes; offsets of + 4 and - 4 both occur.
All inputs are finite; a program needn't handle non-finite values.
Results may differ from a plain program's by a relative error of at most 0.0001.
Values sent between devices are 32-bit elements; how exact they have to be, the bound alone decides.
A program may use at most 64 MiB of HBM per device.

v0:
```python
import jax
import jax.numpy as jnp
from jax import lax
from jax.sharding import PartitionSpec as P

dt_step = 0.1


def extended_2(block, sides, width):
    for axis, dim in sides:
        count = lax.axis_size(axis)
        forward = [(i, i + 1) for i in range(count - 1)]
        forward.append((count - 1, 0))
        backward = [(target, source) for source, target in forward]
        low = lax.ppermute(
            lax.slice_in_dim(block, block.shape[dim] - width, None, axis=dim), axis, forward
        )
        high = lax.ppermute(lax.slice_in_dim(block, 0, width, axis=dim), axis, backward)
        block = jnp.concatenate([low, block, high], axis=dim)
    return block


def spanwise_tables(mode_count, point_count):
    column_ids = jnp.arange(2 * mode_count)
    wavenumber = (column_ids // 2).astype(jnp.float32)
    imag_part = column_ids % 2
    positions = 2.0 * jnp.pi * jnp.arange(point_count).astype(jnp.float32) / point_count
    phases = wavenumber[:, None] * positions[None, :]
    forward = jnp.where(imag_part[:, None] == 0, jnp.cos(phases), -jnp.sin(phases)) / jnp.sqrt(
        jnp.float32(mode_count)
    )
    backward = forward.T * (2.0 * mode_count / point_count)
    return (forward, backward)


def apply_inverse(block, helmholtz, kx_count, ht_count, slots_dev, rows_ht):
    components, reals_dev, band_modes = (block.shape[0], block.shape[1], block.shape[2])
    regrouped = block.reshape(
        components, reals_dev, band_modes, kx_count, ht_count, slots_dev, 2, rows_ht
    )
    regrouped = regrouped.transpose(0, 1, 3, 2, 5, 6, 4, 7)
    regrouped = regrouped.reshape(
        components, reals_dev, kx_count * band_modes, slots_dev, 2, ht_count * rows_ht
    )
    solved = jnp.einsum("syx,crmspx->crmspy", helmholtz, regrouped, precision=lax.Precision.HIGHEST)
    solved = solved.reshape(
        components, reals_dev, kx_count, band_modes, slots_dev, 2, ht_count, rows_ht
    )
    solved = solved.transpose(0, 1, 3, 2, 6, 4, 5, 7)
    return solved.reshape(block.shape)


def local(velocity, low_index, neighbours, owner_map, mode_counts, helmholtz):
    highest = lax.Precision.HIGHEST
    components, reals_dev, band_modes, rows_ht, columns = velocity.shape
    kz_modes = columns // 2
    forward, backward = spanwise_tables(kz_modes, 4 * kz_modes)
    kx_count = lax.axis_size("kx")
    ht_count = lax.axis_size("ht")
    kx_total = band_modes * kx_count
    realizations = reals_dev * lax.axis_size("real")
    owners = kx_count * ht_count
    slots_dev = kz_modes // owners
    width_out = slots_dev * 2 * rows_ht
    low_members = low_index.shape[0]
    band_start = lax.axis_index("kx") * band_modes
    global_modes = band_start + jnp.arange(band_modes, dtype=jnp.int32)
    low_select = (low_index[:, None] == global_modes[None, :]).astype(jnp.float32)
    high_mask = 1.0 - jnp.sum(low_select, axis=0)
    offsets = (neighbours - global_modes[:, None] + kx_total // 2) % kx_total - kx_total // 2
    local_partner = jnp.arange(band_modes, dtype=jnp.int32)[:, None] + band_modes + offsets
    column_mask = ((jnp.arange(columns) // 2)[None, :] < mode_counts[:, None]).astype(jnp.float32)
    inverse_map = (
        jnp.zeros((kz_modes,), jnp.int32).at[owner_map].set(jnp.arange(kz_modes, dtype=jnp.int32))
    )
    current = velocity
    physical = jnp.dot(current, forward, precision=highest)
    extended = extended_2(physical, (("kx", 2),), band_modes)
    own_low = jnp.einsum("jm,crmyz->crjyz", low_select, physical, precision=highest)
    low_fields = lax.psum(own_low, "kx")
    high_low = jnp.zeros_like(physical)
    stresses = []
    for member in range(low_members):
        partner = jnp.take(extended, local_partner[:, member], axis=2)
        low_one = low_fields[:, :, member : member + 1]
        high_low = high_low + low_one * partner[1:2] + partner * low_one[1:2]
        weighted = physical * (partner[1:2] * high_mask[None, None, :, None, None])
        stresses.append(jnp.sum(weighted, axis=(1, 2)))
    stress = jnp.stack(stresses, axis=1)
    nonlinear = jnp.dot(high_low, backward, precision=highest)
    summed = lax.psum(stress, ("kx", "real"))
    low_forcing = jnp.dot(summed / realizations, backward, precision=highest)
    forcing = nonlinear * high_mask[None, None, :, None, None]
    forcing = (
        forcing + jnp.einsum("jm,cjyk->cmyk", low_select, low_forcing, precision=highest)[:, None]
    )
    forcing = forcing * column_mask[None, None, :, None, :]
    updated = current + dt_step * forcing
    slotted = jnp.take(
        updated.reshape(components, reals_dev, band_modes, rows_ht, kz_modes, 2), owner_map, axis=4
    )
    outgoing = slotted.reshape(components, reals_dev, band_modes, rows_ht, owners, slots_dev, 2)
    outgoing = outgoing.transpose(0, 1, 2, 4, 5, 6, 3)
    flat_out = outgoing.reshape(components, reals_dev, band_modes, owners, width_out)
    applied = apply_inverse(
        lax.all_to_all(flat_out, ("kx", "ht"), split_axis=3, concat_axis=3, tiled=True),
        helmholtz,
        kx_count,
        ht_count,
        slots_dev,
        rows_ht,
    )
    returned = lax.all_to_all(applied, ("kx", "ht"), split_axis=3, concat_axis=3, tiled=True)
    restored = returned.reshape(components, reals_dev, band_modes, owners, slots_dev, 2, rows_ht)
    restored = restored.transpose(0, 1, 2, 6, 3, 4, 5).reshape(
        components, reals_dev, band_modes, rows_ht, kz_modes, 2
    )
    current = jnp.take(restored, inverse_map, axis=4).reshape(
        components, reals_dev, band_modes, rows_ht, columns
    )
    return current


def solution(mesh):
    in_specs = (
        P(None, "real", "kx", "ht", None),
        P(),
        P("kx", None),
        P(),
        P("kx"),
        P(("kx", "ht"), None, None),
    )
    out_specs = P(None, "real", "kx", "ht", None)
    return jax.shard_map(local, mesh=mesh, in_specs=in_specs, out_specs=out_specs, check_vma=False)
```

profile of v0, /device:TPU:1, one launch (start us, length us, event | category | flops | bytes accessed | tf_op | source)
XLA Modules:
  0.0 327.1 jit_solution(15920989410416831472)
XLA Ops:
  6.6 2.4 fusion.12
  9.0 2.5 collective-permute-start
  11.5 4.0 %collective-permute-start.1 = (f32[3,1,4,64,256]{4,3,2,0,1:T(8,128)S(1)}, f32[3,1,4,64,256]{4,3,2,0,1:T(8,128)}, u32[]{:S(2)}, u32[]{:S(2)}) collective-permute-start(f32[3,1,4,64,256]{4,3,2,0,1:T(8,128)S(1)} %bitcast.259), channel_id=1, source_target_pairs={{32,0},{64,32},{96,64},{128,96},{160,128},{192,160},{224,192},{0,2... | collective-permute-start | bytes 2359304 | tf_op jit(solution)/shard_map/ppermute | solution.py:18
  15.6 3.1 convolution_bitcast_fusion
  18.9 0.3 slice_reduce_fusion.7
  19.8 12.9 %collective-permute-done = f32[3,1,4,64,256]{4,3,2,0,1:T(8,128)S(1)} collective-permute-done((f32[3,1,4,64,256]{4,3,2,0,1:T(8,128)S(1)}, f32[3,1,4,64,256]{4,3,2,0,1:T(8,128)S(1)}, u32[]{:S(2)}, u32[]{:S(2)}) %collective-permute-start) | collective-permute-done | bytes 786464 | tf_op jit(solution)/shard_map/ppermute | solution.py:15
  32.7 0.9 copy-done.16
  33.6 1.8 maximum_bitcast_fusion
  35.4 1.6 gather_fusion.7
  37.0 1.5 gather_fusion.5
  38.5 1.5 gather_fusion.4
  40.0 1.5 gather_fusion.3
  41.5 1.5 gather_fusion.2
  43.0 1.5 gather_fusion.1
  44.5 1.5 gather_fusion
  46.0 1.5 gather_fusion.6
  47.5 1.4 bitcast_select_fusion.2
  48.9 1.3 bitcast_select_fusion.4
  50.8 0.6 copy-done.10
  52.1 1.4 multiply_bitcast_fusion.1
  53.7 0.5 multiply_reduce_fusion
  55.4 3.9 %stack.35 = f32[3,8,64,256]{3,1,2,0:T(8,128)} concatenate(f32[3,1,64,256]{3,1,2,0:T(1,128)S(1)} %stack.27, f32[3,1,64,256]{3,1,2,0:T(1,128)S(1)} %stack.28, f32[3,1,64,256]{3,1,2,0:T(1,128)S(1)} %stack.29, f32[3,1,64,256]{3,1,2,0:T(1,128)S(1)} %stack.30, f32[3,1,64,256]{3,1,2,0:T(1,128)S(1)} %stack.31, f32[3,1,64,256]{3,1,2,0:T(1,128)S(1)} %stack.32, ...), dimensions={1} | concatenate | bytes 3145728 | tf_op jit(solution)/shard_map/stack | solution.py:89
  59.3 0.5 copy-done.31
  59.8 0.5 compare_and_fusion.1
  60.4 35.1 %all-reduce.3.cloned.1.call-done = f32[3,1,8,64,256]{4,2,3,0,1:T(8,128)} async-done(((f32[3,1,8,64,256]{4,2,3,0,1:T(8,128)}), f32[3,1,8,64,256]{4,2,3,0,1:T(8,128)}) %all-reduce.3.cloned.1.call-update) | async-done | bytes 1572880 | tf_op jit(solution)/shard_map/psum | solution.py:80
  95.5 7.7 %fusion.51 = (f32[3,1,1,64,256]{4,2,3,0,1:T(1,128)S(1)}, f32[3,1,1,64,256]{4,2,3,0,1:T(1,128)S(1)}, f32[3,1,1,64,256]{4,2,3,0,1:T(1,128)S(1)}, f32[3,1,1,64,256]...) fusion(f32[3,1,8,64,256]{4,2,3,0,1:T(8,128)} %all-reduce.3.clon, ...), kind=kLoop, calls=%fused_computation.172 | loop fusion | bytes 3145728 | tf_op jit(solution)/shard_map/slice | solution.py:85
  103.2 0.7 copy.102
  103.8 0.7 copy.103
  104.5 0.7 copy.104
  105.2 0.7 copy.105
  105.9 0.7 copy.106
  106.6 0.7 copy.107
  107.3 0.7 copy.108
  108.0 0.7 copy.109
  108.7 3.5 %fusion.52 = (f32[1,1,1,64,256]{4,2,3,0,1:T(1,128)S(1)}, f32[1,1,1,64,256]{4,2,3,0,1:T(1,128)S(1)}, f32[1,1,1,64,256]{4,2,3,0,1:T(1,128)S(1)}, f32[1,1,1,64,256]...) fusion(f32[3,1,8,64,256]{4,2,3,0,1:T(8,128)} %all-reduce.3.clon, ...), kind=kLoop, calls=%fused_computation.173 | loop fusion | bytes 1048576 | tf_op jit(solution)/shard_map/slice | solution.py:86
  112.2 0.6 copy.112
  112.8 0.6 copy.113
  113.5 0.6 copy.114
  114.1 0.6 copy.115
  114.7 0.6 copy.116
  115.3 0.6 copy.117
  116.0 133.7 %all-reduce.5.cloned.1.call-done = f32[3,8,64,256]{3,1,2,0:T(8,128)} async-done(((f32[3,8,64,256]{3,1,2,0:T(8,128)}), f32[3,8,64,256]{3,1,2,0:T(8,128)}) %all-reduce.5.cloned.1.call-update) | async-done | bytes 1572880 | tf_op jit(solution)/shard_map/psum | solution.py:91
  249.7 3.5 %fusion = f32[3,8,64,128]{3,1,2,0:T(8,128)S(1)} fusion(f32[3,8,64,256]{3,1,2,0:T(8,128)} %all-reduce.5.cloned.1.call-done, f32[256]{0:T(256)S(1)} %convert_multiply_fusion, f32[128]{0:T(128)} %copy-done.17, pred[128]{0:T(512)(128)(4,1)S(1)} %fusion.42), kind=kOutput, calls=%fused_computation.12 | convolution fusion | flops 604504064 | bytes 2360960 | tf_op jit(solution)/shard_map/dot_general | solution.py:92
  253.2 1.2 fusion.50
  254.4 5.9 %fusion.6 = f32[3,1,4,64,128]{4,3,2,0,1:T(8,128)} fusion(f32[3,1,4,64,128]{4,3,2,1,0:T(8,128)S(1)} %copy-done.14, f32[3,64,128,4]{2,3,1,0:T(4,128)S(1)} %fusion.50, f32[4,128]{1,0:T(4,128)S(1)} %compare_convert_fusion.1, f32[4]{0:T(128)} %copy-done.27, f32[256]{0:T(256)S(1)} %convert_multiply_fusion, f32[128]{0:T(128)} %copy-done.17, ...), kind=kOutput, calls=%fused_computation.21 | convolution fusion | flops 310280192 | bytes 11669168 | tf_op jit(solution)/shard_map/dot_general | solution.py:90
  260.3 1.3 copy.38
  261.6 0.5 copy.101
  262.1 1.0 gather_fusion.8
  263.2 0.2 fusion.7
  263.4 0.4 copy.55
  263.8 0.6 reshape.457
  264.4 27.5 %all_to_all.10 = f32[3,1,4,64,128]{4,2,0,1,3:T(4,128)S(1)} all-to-all(f32[3,1,4,64,128]{4,2,0,1,3:T(4,128)S(1)} %reshape.457), channel_id=1, replica_groups=mesh['kx'=8,'ht'=8,'real'=4] {'kx','ht'}, dimensions={3} | all-to-all | bytes 786432 | tf_op jit(solution)/shard_map/all_to_all | solution.py:106
  292.0 0.5 reshape.287
  292.8 1.5 convolution_bitcast_fusion.1
  294.3 0.6 copy.56
  294.9 1.3 reshape.459
  296.2 5.5 %all-to-all-start.1 = ((f32[3,1,4,64,128]{4,2,0,1,3:T(4,128)}), f32[3,1,4,64,128]{4,2,0,1,3:T(4,128)S(1)}, u32[]{:S(2)}, u32[]{:S(2)}) async-start(f32[3,1,4,64,128]{4,2,0,1,3:T(4,128)} %reshape.459), calls=%async_computation.1 | async-start | bytes 786432 | tf_op jit(solution)/shard_map/all_to_all | solution.py:113
  301.6 0.9 scatter_custom_fusion
  302.6 14.2 %all-to-all-done.1 = f32[3,1,4,64,128]{4,2,0,1,3:T(4,128)S(1)} async-done(((f32[3,1,4,64,128]{4,2,0,1,3:T(4,128)}), f32[3,1,4,64,128]{4,2,0,1,3:T(4,128)S(1)}, u32[]{:S(2)}, u32[]{:S(2)}) %all-to-all-start.1) | async-done | bytes 393248 | tf_op jit(solution)/shard_map/all_to_all | solution.py:113
  316.8 0.5 reshape.460
  317.5 1.1 gather_fusion.9
  318.6 0.2 bitcast_select_fusion
  318.8 0.4 copy.48
  319.3 1.0 copy.49
  (129 shorter events, 3.6 us)
Async XLA Ops:
  6.5 286.2 %copy-start = (f32[1,512,512]{2,1,0:T(8,128)S(1)}, f32[1,512,512]{2,1,0:T(8,128)}, u32[]{:S(2)}) copy-start(f32[1,512,512]{2,1,0:T(8,128)} %param.15) | copy-start | bytes 3145732
  6.5 89.0 %all-reduce.3.cloned.1.call-start = ((), (), s32[]{:S(2)}) async-start(), calls=%async_computation.2 | async-start | bytes 3145728 | tf_op jit(solution)/shard_map/psum | solution.py:80
  6.6 12.2 %copy-start.17 = (f32[128]{0:T(128)}, f32[128]{0:T(128)S(1)}, u32[]{:S(2)}) copy-start(f32[128]{0:T(128)S(1)} %fusion.45) | copy-start | bytes 1540
  6.6 12.2 %copy-start.28 = (s32[4,8]{1,0:T(4,128)S(1)}, s32[4,8]{1,0:T(4,128)}, u32[]{:S(2)}) copy-start(s32[4,8]{1,0:T(4,128)} %param.12) | copy-start | bytes 388
  6.6 13.0 %copy-start.29 = (s32[8]{0:T(128)S(1)}, s32[8]{0:T(128)}, u32[]{:S(2)}) copy-start(s32[8]{0:T(128)} %param.11) | copy-start | bytes 100
  9.0 23.7 %copy-start.1 = (f32[256,3,4,64]{0,3,2,1:T(8,128)}, f32[256,3,4,64]{0,3,2,1:T(8,128)S(1)}, u32[]{:S(2)}) copy-start(f32[256,3,4,64]{0,3,2,1:T(8,128)S(1)} %fusion.12) | copy-start | bytes 2359300
  9.0 23.7 %collective-permute-start = (f32[3,1,4,64,256]{4,3,2,0,1:T(8,128)S(1)}, f32[3,1,4,64,256]{4,3,2,0,1:T(8,128)S(1)}, u32[]{:S(2)}, u32[]{:S(2)}) collective-permute-start(f32[3,1,4,64,256]{4,3,2,0,1:T(8,128)S(1)} %bitcast.258), channel_id=1, source_target_pairs={{0,32},{32,64},{64,96},{96,128},{128,160},{160,192},{192,224},{224... | collective-permute-start | bytes 2359304 | tf_op jit(solution)/shard_map/ppermute | solution.py:15
  11.5 22.1 %collective-permute-start.1 = (f32[3,1,4,64,256]{4,3,2,0,1:T(8,128)S(1)}, f32[3,1,4,64,256]{4,3,2,0,1:T(8,128)}, u32[]{:S(2)}, u32[]{:S(2)}) collective-permute-start(f32[3,1,4,64,256]{4,3,2,0,1:T(8,128)S(1)} %bitcast.259), channel_id=1, source_target_pairs={{32,0},{64,32},{96,64},{128,96},{160,128},{192,160},{224,192},{0,2... | collective-permute-start | bytes 2359304 | tf_op jit(solution)/shard_map/ppermute | solution.py:18
  15.6 19.9 %copy-start.18 = (s32[4]{0:T(128)}, s32[4]{0:T(128)S(1)}, u32[]{:S(2)}) copy-start(s32[4]{0:T(128)S(1)} %get-tuple-element.70) | copy-start | bytes 52
  18.8 230.9 %all-reduce.5.cloned.1.call-start = ((), (), s32[]{:S(2)}) async-start(), calls=%async_computation.3 | async-start | bytes 3145728 | tf_op jit(solution)/shard_map/psum | solution.py:91
  19.2 28.2 %copy-start.19 = (pred[4]{0:T(512)(128)(4,1)}, pred[4]{0:T(512)(128)(4,1)S(1)}, u32[]{:S(2)}) copy-start(pred[4]{0:T(512)(128)(4,1)S(1)} %compare_and_fusion.2) | copy-start | bytes 16
  19.3 29.6 %copy-start.20 = (pred[4]{0:T(512)(128)(4,1)}, pred[4]{0:T(512)(128)(4,1)S(1)}, u32[]{:S(2)}) copy-start(pred[4]{0:T(512)(128)(4,1)S(1)} %compare_and_fusion.4) | copy-start | bytes 16
  19.3 30.9 %copy-start.21 = (pred[4]{0:T(512)(128)(4,1)}, pred[4]{0:T(512)(128)(4,1)S(1)}, u32[]{:S(2)}) copy-start(pred[4]{0:T(512)(128)(4,1)S(1)} %compare_and_fusion.5) | copy-start | bytes 16
  19.3 31.1 %copy-start.22 = (pred[4]{0:T(512)(128)(4,1)}, pred[4]{0:T(512)(128)(4,1)S(1)}, u32[]{:S(2)}) copy-start(pred[4]{0:T(512)(128)(4,1)S(1)} %compare_and_fusion.6) | copy-start | bytes 16
  19.4 31.2 %copy-start.23 = (pred[4]{0:T(512)(128)(4,1)}, pred[4]{0:T(512)(128)(4,1)S(1)}, u32[]{:S(2)}) copy-start(pred[4]{0:T(512)(128)(4,1)S(1)} %compare_and_fusion.7) | copy-start | bytes 16
  19.4 31.4 %copy-start.24 = (pred[4]{0:T(512)(128)(4,1)}, pred[4]{0:T(512)(128)(4,1)S(1)}, u32[]{:S(2)}) copy-start(pred[4]{0:T(512)(128)(4,1)S(1)} %compare_and_fusion.8) | copy-start | bytes 16
  19.7 31.8 %copy-start.25 = (pred[4]{0:T(512)(128)(4,1)}, pred[4]{0:T(512)(128)(4,1)S(1)}, u32[]{:S(2)}) copy-start(pred[4]{0:T(512)(128)(4,1)S(1)} %compare_and_fusion.9) | copy-start | bytes 16
  19.8 32.1 %copy-start.26 = (pred[4]{0:T(512)(128)(4,1)}, pred[4]{0:T(512)(128)(4,1)S(1)}, u32[]{:S(2)}) copy-start(pred[4]{0:T(512)(128)(4,1)S(1)} %compare_and_fusion.3) | copy-start | bytes 16
  19.8 32.3 %copy-start.27 = (f32[4]{0:T(128)}, f32[4]{0:T(128)S(1)}, u32[]{:S(2)}) copy-start(f32[4]{0:T(128)S(1)} %broadcast_subtract_fusion) | copy-start | bytes 52
  32.7 0.9 copy-start.16
  47.5 2.8 copy-start.5
  47.5 3.0 copy-start.6
  48.9 1.7 copy-start.8
  50.3 1.2 copy-start.10
  50.4 1.2 copy-start.12
  50.6 1.4 copy-start.13
  52.1 1.6 copy-start.2
  55.3 3.9 %copy-start.33 = (s32[64]{0:T(128)S(1)}, s32[64]{0:T(128)}, u32[]{:S(2)}) copy-start(s32[64]{0:T(128)} %param.13) | copy-start | bytes 772
  55.4 5.0 %copy-start.32 = (s32[4]{0:T(128)S(1)}, s32[4]{0:T(128)}, u32[]{:S(2)}) copy-start(s32[4]{0:T(128)} %param.14) | copy-start | bytes 52
  59.3 0.5 copy-start.31
  112.2 142.2 %copy-start.3 = (f32[4,3,64,256]{3,2,1,0:T(8,128)S(1)}, f32[4,3,64,256]{3,2,1,0:T(8,128)}, u32[]{:S(2)}) copy-start(f32[4,3,64,256]{3,2,1,0:T(8,128)} %gather_fusion.7) | copy-start | bytes 2359300
  112.2 142.2 %copy-start.4 = (f32[4,3,64,256]{3,2,1,0:T(8,128)S(1)}, f32[4,3,64,256]{3,2,1,0:T(8,128)}, u32[]{:S(2)}) copy-start(f32[4,3,64,256]{3,2,1,0:T(8,128)} %gather_fusion.5) | copy-start | bytes 2359300
  249.7 4.7 %copy-start.7 = (f32[4,3,64,256]{3,2,1,0:T(8,128)S(1)}, f32[4,3,64,256]{3,2,1,0:T(8,128)}, u32[]{:S(2)}) copy-start(f32[4,3,64,256]{3,2,1,0:T(8,128)} %gather_fusion.3) | copy-start | bytes 2359300
  249.7 4.7 %copy-start.9 = (f32[4,3,64,256]{3,2,1,0:T(8,128)S(1)}, f32[4,3,64,256]{3,2,1,0:T(8,128)}, u32[]{:S(2)}) copy-start(f32[4,3,64,256]{3,2,1,0:T(8,128)} %gather_fusion.2) | copy-start | bytes 2359300
  249.7 4.7 %copy-start.11 = (f32[4,3,64,256]{3,2,1,0:T(8,128)S(1)}, f32[4,3,64,256]{3,2,1,0:T(8,128)}, u32[]{:S(2)}) copy-start(f32[4,3,64,256]{3,2,1,0:T(8,128)} %gather_fusion.1) | copy-start | bytes 2359300
  249.7 4.7 %copy-start.14 = (f32[3,1,4,64,128]{4,3,2,1,0:T(8,128)S(1)}, f32[3,1,4,64,128]{4,3,2,1,0:T(8,128)}, u32[]{:S(2)}) copy-start(f32[3,1,4,64,128]{4,3,2,1,0:T(8,128)} %param.10) | copy-start | bytes 1179652
  249.7 4.7 %copy-start.15 = (f32[4,64,256]{2,1,0:T(8,128)S(1)}, f32[4,64,256]{2,1,0:T(8,128)}, u32[]{:S(2)}) copy-start(f32[4,64,256]{2,1,0:T(8,128)} %get-tuple-element.40) | copy-start | bytes 786436
  262.1 1.1 copy-start.30
  296.2 20.6 %all-to-all-start.1 = ((f32[3,1,4,64,128]{4,2,0,1,3:T(4,128)}), f32[3,1,4,64,128]{4,2,0,1,3:T(4,128)S(1)}, u32[]{:S(2)}, u32[]{:S(2)}) async-start(f32[3,1,4,64,128]{4,2,0,1,3:T(4,128)} %reshape.459), calls=%async_computation.1 | async-start | bytes 786432 | tf_op jit(solution)/shard_map/all_to_all | solution.py:113
Sparse Core Ops, SparseCore 0:
  18.9 76.5 all-reduce.2
  98.9 150.7 all-reduce.4
where the time goes:
time: 328 us; the launch traced here: 327 us
  waiting for transfers between devices  196 us (60%)
  local copies, waits for them, and re-layouts  50.8 us (15%)
  blocking collectives  27.5 us (8%)
  matrix products  17.6 us (5%)
  between operations  14.4 us (4%)
  starting transfers between devices  12.1 us (4%)
  other arithmetic  8.77 us (3%)
    psum x1, waiting for transfers between devices, local(): summed = lax.psum(stress, ('kx', 'real'))  134 us
    psum x1, waiting for transfers between devices, local(): low_fields = lax.psum(own_low, 'kx')  35.1 us
    all_to_all x1, blocking collectives, local(): lax.all_to_all(flat_out, ('kx', 'ht'), split_axis=3, concat_axis=3, tiled...  27.5 us
    all_to_all x1, waiting for transfers between devices, local(): lax.all_to_all(applied, ('kx', 'ht'), split_axis=3, concat_axis=3, tiled=...  14.2 us
    ppermute x1, waiting for transfers between devices, extended_2(): lax.ppermute(lax.slice_in_dim(block, block.shape[dim] - width, None, axis...  12.9 us
    gather x8, local copies, waits for them, and re-layouts, local(): partner = jnp.take(extended, local_partner[:, member], axis=2)  12 us
    unnamed x84, local copies, waits for them, and re-layouts  11.8 us
    slice x1, local copies, waits for them, and re-layouts, local(): low_one = low_fields[:, :, member:member + 1]  7.67 us
  transfers between devices with their start and end apart: 5, of which 4 were waited for; matrix products, arithmetic and copies ran while one was open for 15% of the time, Pallas kernels for 0%

commit v1 on v0

--- a/solution.py
+++ b/solution.py
@@ -110,7 +110,12 @@
         slots_dev,
         rows_ht,
     )
-    returned = lax.all_to_all(applied, ("kx", "ht"), split_axis=3, concat_axis=3, tiled=True)
+    returned = jnp.concatenate(
+        lax.all_to_all(
+            jnp.stack(jnp.split(applied, lax.axis_size(("kx", "ht")), axis=3)), ("kx", "ht"), 0, 0
+        ),
+        axis=3,
+    )
     restored = returned.reshape(components, reals_dev, band_modes, owners, slots_dev, 2, rows_ht)
     restored = restored.transpose(0, 1, 2, 6, 3, 4, 5).reshape(
         components, reals_dev, band_modes, rows_ht, kz_modes, 2

time: 328 us -> 365 us (1.11)
  local copies, waits for them, and re-layouts: 50.8 us -> 87.6 us
    unnamed x84 -> x151, local copies, waits for them, and re-layouts: 11.8 us -> 48.8 us
  transfers between devices with their start and end apart: 5 -> 5, of which waited for: 4 -> 4; matrix products, arithmetic and copies ran while one was open for 15% -> 14% of each run, Pallas kernels for 0% -> 0%
where the time goes in v1:
time: 365 us; the launch traced here: 364 us
  waiting for transfers between devices  196 us (54%)
  local copies, waits for them, and re-layouts  87.6 us (24%)
  blocking collectives  27.5 us (8%)
  matrix products  17.6 us (5%)
  between operations  14.5 us (4%)
  starting transfers between devices  12.1 us (3%)
  other arithmetic  8.73 us (2%)
    psum x1, waiting for transfers between devices, local(): summed = lax.psum(stress, ('kx', 'real'))  134 us
    unnamed x151, local copies, waits for them, and re-layouts  48.8 us
    psum x1, waiting for transfers between devices, local(): low_fields = lax.psum(own_low, 'kx')  34.3 us
    all_to_all x1, blocking collectives, local(): lax.all_to_all(flat_out, ('kx', 'ht'), split_axis=3, concat_axis=3, tiled...  27.5 us
    all_to_all x1, waiting for transfers between devices, local(): lax.all_to_all(jnp.stack(jnp.split(applied, lax.axis_size(('kx', 'ht')),...  15.1 us
    ppermute x1, waiting for transfers between devices, extended_2(): lax.ppermute(lax.slice_in_dim(block, block.shape[dim] - width, None, axis...  12.9 us
    gather x8, local copies, waits for them, and re-layouts, local(): partner = jnp.take(extended, local_partner[:, member], axis=2)  12 us
    slice x1, local copies, waits for them, and re-layouts, local(): low_one = low_fields[:, :, member:member + 1]  7.67 us
  transfers between devices with their start and end apart: 5, of which 4 were waited for; matrix products, arithmetic and copies ran while one was open for 14% of the time, Pallas kernels for 0%

profile of v1, /device:TPU:1, one launch (start us, length us, event | category | flops | bytes accessed | tf_op | source)
XLA Modules:
  0.0 364.1 jit_solution(2653898044586742558)
XLA Ops:
  6.6 2.4 fusion.12
  9.1 2.5 collective-permute-start
  11.6 4.0 %collective-permute-start.1 = (f32[3,1,4,64,256]{4,3,2,0,1:T(8,128)S(1)}, f32[3,1,4,64,256]{4,3,2,0,1:T(8,128)}, u32[]{:S(2)}, u32[]{:S(2)}) collective-permute-start(f32[3,1,4,64,256]{4,3,2,0,1:T(8,128)S(1)} %bitcast.450), channel_id=1, source_target_pairs={{32,0},{64,32},{96,64},{128,96},{160,128},{192,160},{224,192},{0,2... | collective-permute-start | bytes 2359304 | tf_op jit(solution)/shard_map/ppermute | solution.py:18
  15.6 3.1 convolution_bitcast_fusion
  19.8 12.9 %collective-permute-done = f32[3,1,4,64,256]{4,3,2,0,1:T(8,128)S(1)} collective-permute-done((f32[3,1,4,64,256]{4,3,2,0,1:T(8,128)S(1)}, f32[3,1,4,64,256]{4,3,2,0,1:T(8,128)S(1)}, u32[]{:S(2)}, u32[]{:S(2)}) %collective-permute-start) | collective-permute-done | bytes 786464 | tf_op jit(solution)/shard_map/ppermute | solution.py:15
  32.8 0.9 copy-done.16
  33.7 1.8 maximum_bitcast_fusion
  35.5 1.6 gather_fusion.7
  37.0 1.5 gather_fusion.5
  38.6 1.5 gather_fusion.4
  40.1 1.5 gather_fusion.3
  41.5 1.5 gather_fusion.2
  43.1 1.5 gather_fusion.1
  44.5 1.5 gather_fusion
  46.0 1.5 gather_fusion.6
  47.5 1.4 bitcast_select_fusion.2
  48.9 1.3 bitcast_select_fusion.4
  50.8 0.6 copy-done.10
  52.2 1.4 multiply_bitcast_fusion.1
  55.4 3.7 %stack.230 = f32[3,8,64,256]{3,1,2,0:T(8,128)} concatenate(f32[3,1,64,256]{3,1,2,0:T(1,128)S(1)} %stack.222, f32[3,1,64,256]{3,1,2,0:T(1,128)S(1)} %stack.223, f32[3,1,64,256]{3,1,2,0:T(1,128)S(1)} %stack.224, f32[3,1,64,256]{3,1,2,0:T(1,128)S(1)} %stack.225, f32[3,1,64,256]{3,1,2,0:T(1,128)S(1)} %stack.226, f32[3,1,64,256]{3,1,2,0:T(1,128)S(1)} %stack.227, ...), dimensions={1} | concatenate | bytes 3145728 | tf_op jit(solution)/shard_map/stack | solution.py:89
  59.1 1.0 scatter_custom_fusion
  60.7 34.3 %all-reduce.3.cloned.1.call-done = f32[3,1,8,64,256]{4,2,3,0,1:T(8,128)} async-done(((f32[3,1,8,64,256]{4,2,3,0,1:T(8,128)}), f32[3,1,8,64,256]{4,2,3,0,1:T(8,128)}) %all-reduce.3.cloned.1.call-update) | async-done | bytes 1572880 | tf_op jit(solution)/shard_map/psum | solution.py:80
  95.0 7.7 %fusion.51 = (f32[3,1,1,64,256]{4,2,3,0,1:T(1,128)S(1)}, f32[3,1,1,64,256]{4,2,3,0,1:T(1,128)S(1)}, f32[3,1,1,64,256]{4,2,3,0,1:T(1,128)S(1)}, f32[3,1,1,64,256]...) fusion(f32[3,1,8,64,256]{4,2,3,0,1:T(8,128)} %all-reduce.3.clon, ...), kind=kLoop, calls=%fused_computation.236 | loop fusion | bytes 3145728 | tf_op jit(solution)/shard_map/slice | solution.py:85
  102.7 0.7 copy.415
  103.4 0.7 copy.416
  104.0 0.7 copy.417
  104.7 0.7 copy.418
  105.4 0.7 copy.419
  106.1 0.7 copy.420
  106.8 0.7 copy.421
  107.5 0.7 copy.422
  108.2 3.5 fusion.52
  111.7 0.6 copy.425
  112.3 0.6 copy.426
  113.0 0.6 copy.427
  113.6 0.6 copy.428
  114.2 0.6 copy.429
  114.8 0.6 copy.430
  115.5 133.7 %all-reduce.5.cloned.1.call-done = f32[3,8,64,256]{3,1,2,0:T(8,128)} async-done(((f32[3,8,64,256]{3,1,2,0:T(8,128)}), f32[3,8,64,256]{3,1,2,0:T(8,128)}) %all-reduce.5.cloned.1.call-update) | async-done | bytes 1572880 | tf_op jit(solution)/shard_map/psum | solution.py:91
  249.2 3.5 fusion
  252.7 1.2 fusion.50
  254.0 5.9 %fusion.6 = f32[3,1,4,64,128]{4,3,2,0,1:T(8,128)} fusion(f32[3,1,4,64,128]{4,3,2,1,0:T(8,128)S(1)} %copy-done.14, f32[3,64,128,4]{2,3,1,0:T(4,128)S(1)} %fusion.50, f32[4,128]{1,0:T(4,128)S(1)} %compare_convert_fusion.1, f32[4]{0:T(128)} %copy-done.28, f32[256]{0:T(256)S(1)} %convert_multiply_fusion, f32[128]{0:T(128)} %copy-done.18, ...), kind=kOutput, calls=%fused_computation.21 | convolution fusion | flops 310280192 | bytes 11669168 | tf_op jit(solution)/shard_map/dot_general | solution.py:90
  259.9 1.3 copy.228
  261.7 1.0 gather_fusion.8
  264.0 27.5 %all_to_all.10 = f32[3,1,4,64,128]{4,2,0,1,3:T(4,128)S(1)} all-to-all(f32[3,1,4,64,128]{4,2,0,1,3:T(4,128)S(1)} %reshape.457), channel_id=1, replica_groups=mesh['kx'=8,'ht'=8,'real'=4] {'kx','ht'}, dimensions={3} | all-to-all | bytes 786432 | tf_op jit(solution)/shard_map/all_to_all | solution.py:106
  292.3 1.5 convolution_bitcast_fusion.1
  293.8 0.6 copy.234
  295.2 0.6 constant_dynamic-update-slice_fusion.63
  302.3 0.6 constant_dynamic-update-slice_fusion.51
  303.5 0.6 constant_dynamic-update-slice_fusion.49
  304.7 0.6 constant_dynamic-update-slice_fusion.47
  305.9 0.6 constant_dynamic-update-slice_fusion.45
  313.6 0.6 constant_dynamic-update-slice_fusion.32
  314.8 0.6 constant_dynamic-update-slice_fusion.30
  316.0 0.6 constant_dynamic-update-slice_fusion.28
  317.2 0.6 constant_dynamic-update-slice_fusion.26
  324.9 0.6 constant_dynamic-update-slice_fusion.13
  326.1 0.6 constant_dynamic-update-slice_fusion.11
  327.3 0.6 constant_dynamic-update-slice_fusion.9
  328.5 0.6 constant_dynamic-update-slice_fusion.7
  333.2 5.4 %all-to-all-start.1 = ((f32[64,3,1,4,1,128]{5,3,1,4,2,0:T(4,128)}), f32[64,3,1,4,1,128]{5,3,1,4,2,0:T(4,128)S(1)}, u32[]{:S(2)}, u32[]{:S(2)}) async-start(f32[64,3,1,4,1,128]{5,3,1,4,2,0:T(4,128)} %constant_dynamic-update-slice_fusion), calls=%async_computation.1 | async-start | bytes 786432 | tf_op jit(solution)/shard_map/all_to_all | solution.py:114
  338.7 15.1 %all-to-all-done.1 = f32[64,3,1,4,1,128]{5,3,1,4,2,0:T(4,128)S(1)} async-done(((f32[64,3,1,4,1,128]{5,3,1,4,2,0:T(4,128)}), f32[64,3,1,4,1,128]{5,3,1,4,2,0:T(4,128)S(1)}, u32[]{:S(2)}, u32[]{:S(2)}) %all-to-all-start.1) | async-done | bytes 393248 | tf_op jit(solution)/shard_map/all_to_all | solution.py:114
  354.6 1.1 gather_fusion.9
  356.3 1.0 copy.301
  (200 shorter events, 39.3 us)
Async XLA Ops:
  6.5 285.8 %copy-start = (f32[1,512,512]{2,1,0:T(8,128)S(1)}, f32[1,512,512]{2,1,0:T(8,128)}, u32[]{:S(2)}) copy-start(f32[1,512,512]{2,1,0:T(8,128)} %param.15) | copy-start | bytes 3145732
  6.5 88.5 %all-reduce.3.cloned.1.call-start = ((), (), s32[]{:S(2)}) async-start(), calls=%async_computation.2 | async-start | bytes 3145728 | tf_op jit(solution)/shard_map/psum | solution.py:80
  6.6 2.5 copy-start.17
  6.6 2.5 copy-start.18
  6.6 12.3 %copy-start.29 = (s32[4,8]{1,0:T(4,128)S(1)}, s32[4,8]{1,0:T(4,128)}, u32[]{:S(2)}) copy-start(s32[4,8]{1,0:T(4,128)} %param.12) | copy-start | bytes 388
  6.6 13.0 %copy-start.30 = (s32[8]{0:T(128)S(1)}, s32[8]{0:T(128)}, u32[]{:S(2)}) copy-start(s32[8]{0:T(128)} %param.11) | copy-start | bytes 100
  6.6 13.2 %copy-start.33 = (s32[64]{0:T(128)S(1)}, s32[64]{0:T(128)}, u32[]{:S(2)}) copy-start(s32[64]{0:T(128)} %param.13) | copy-start | bytes 772
  9.0 23.7 %copy-start.1 = (f32[256,3,4,64]{0,3,2,1:T(8,128)}, f32[256,3,4,64]{0,3,2,1:T(8,128)S(1)}, u32[]{:S(2)}) copy-start(f32[256,3,4,64]{0,3,2,1:T(8,128)S(1)} %fusion.12) | copy-start | bytes 2359300
  9.1 23.7 %collective-permute-start = (f32[3,1,4,64,256]{4,3,2,0,1:T(8,128)S(1)}, f32[3,1,4,64,256]{4,3,2,0,1:T(8,128)S(1)}, u32[]{:S(2)}, u32[]{:S(2)}) collective-permute-start(f32[3,1,4,64,256]{4,3,2,0,1:T(8,128)S(1)} %bitcast.449), channel_id=1, source_target_pairs={{0,32},{32,64},{64,96},{96,128},{128,160},{160,192},{192,224},{224... | collective-permute-start | bytes 2359304 | tf_op jit(solution)/shard_map/ppermute | solution.py:15
  11.6 22.1 %collective-permute-start.1 = (f32[3,1,4,64,256]{4,3,2,0,1:T(8,128)S(1)}, f32[3,1,4,64,256]{4,3,2,0,1:T(8,128)}, u32[]{:S(2)}, u32[]{:S(2)}) collective-permute-start(f32[3,1,4,64,256]{4,3,2,0,1:T(8,128)S(1)} %bitcast.450), channel_id=1, source_target_pairs={{32,0},{64,32},{96,64},{128,96},{160,128},{192,160},{224,192},{0,2... | collective-permute-start | bytes 2359304 | tf_op jit(solution)/shard_map/ppermute | solution.py:18
  15.6 19.9 %copy-start.19 = (s32[4]{0:T(128)}, s32[4]{0:T(128)S(1)}, u32[]{:S(2)}) copy-start(s32[4]{0:T(128)S(1)} %get-tuple-element.134) | copy-start | bytes 52
  18.8 230.4 %all-reduce.5.cloned.1.call-start = ((), (), s32[]{:S(2)}) async-start(), calls=%async_computation.3 | async-start | bytes 3145728 | tf_op jit(solution)/shard_map/psum | solution.py:91
  19.3 28.2 %copy-start.20 = (pred[4]{0:T(512)(128)(4,1)}, pred[4]{0:T(512)(128)(4,1)S(1)}, u32[]{:S(2)}) copy-start(pred[4]{0:T(512)(128)(4,1)S(1)} %compare_and_fusion.2) | copy-start | bytes 16
  19.3 29.6 %copy-start.21 = (pred[4]{0:T(512)(128)(4,1)}, pred[4]{0:T(512)(128)(4,1)S(1)}, u32[]{:S(2)}) copy-start(pred[4]{0:T(512)(128)(4,1)S(1)} %compare_and_fusion.4) | copy-start | bytes 16
  19.3 31.0 %copy-start.22 = (pred[4]{0:T(512)(128)(4,1)}, pred[4]{0:T(512)(128)(4,1)S(1)}, u32[]{:S(2)}) copy-start(pred[4]{0:T(512)(128)(4,1)S(1)} %compare_and_fusion.5) | copy-start | bytes 16
  19.4 31.1 %copy-start.23 = (pred[4]{0:T(512)(128)(4,1)}, pred[4]{0:T(512)(128)(4,1)S(1)}, u32[]{:S(2)}) copy-start(pred[4]{0:T(512)(128)(4,1)S(1)} %compare_and_fusion.6) | copy-start | bytes 16
  19.4 31.2 %copy-start.24 = (pred[4]{0:T(512)(128)(4,1)}, pred[4]{0:T(512)(128)(4,1)S(1)}, u32[]{:S(2)}) copy-start(pred[4]{0:T(512)(128)(4,1)S(1)} %compare_and_fusion.7) | copy-start | bytes 16
  19.4 31.4 %copy-start.25 = (pred[4]{0:T(512)(128)(4,1)}, pred[4]{0:T(512)(128)(4,1)S(1)}, u32[]{:S(2)}) copy-start(pred[4]{0:T(512)(128)(4,1)S(1)} %compare_and_fusion.8) | copy-start | bytes 16
  19.5 32.1 %copy-start.26 = (pred[4]{0:T(512)(128)(4,1)}, pred[4]{0:T(512)(128)(4,1)S(1)}, u32[]{:S(2)}) copy-start(pred[4]{0:T(512)(128)(4,1)S(1)} %compare_and_fusion.9) | copy-start | bytes 16
  19.8 32.1 %copy-start.27 = (pred[4]{0:T(512)(128)(4,1)}, pred[4]{0:T(512)(128)(4,1)S(1)}, u32[]{:S(2)}) copy-start(pred[4]{0:T(512)(128)(4,1)S(1)} %compare_and_fusion.3) | copy-start | bytes 16
  19.8 32.3 %copy-start.28 = (f32[4]{0:T(128)}, f32[4]{0:T(128)S(1)}, u32[]{:S(2)}) copy-start(f32[4]{0:T(128)S(1)} %broadcast_subtract_fusion) | copy-start | bytes 52
  32.8 0.9 copy-start.16
  47.5 2.8 copy-start.5
  47.5 3.0 copy-start.6
  48.9 1.7 copy-start.8
  50.3 1.2 copy-start.10
  50.5 1.2 copy-start.12
  50.7 1.4 copy-start.13
  52.2 1.6 copy-start.2
  55.4 5.2 %copy-start.32 = (s32[4]{0:T(128)S(1)}, s32[4]{0:T(128)}, u32[]{:S(2)}) copy-start(s32[4]{0:T(128)} %param.14) | copy-start | bytes 52
  60.1 45.3 %copy-start.34 = (s32[64]{0:T(128)}, s32[64]{0:T(128)S(1)}, u32[]{:S(2)}) copy-start(s32[64]{0:T(128)S(1)} %scatter_custom_fusion) | copy-start | bytes 772
  111.7 142.3 %copy-start.3 = (f32[4,3,64,256]{3,2,1,0:T(8,128)S(1)}, f32[4,3,64,256]{3,2,1,0:T(8,128)}, u32[]{:S(2)}) copy-start(f32[4,3,64,256]{3,2,1,0:T(8,128)} %gather_fusion.7) | copy-start | bytes 2359300
  111.7 142.3 %copy-start.4 = (f32[4,3,64,256]{3,2,1,0:T(8,128)S(1)}, f32[4,3,64,256]{3,2,1,0:T(8,128)}, u32[]{:S(2)}) copy-start(f32[4,3,64,256]{3,2,1,0:T(8,128)} %gather_fusion.5) | copy-start | bytes 2359300
  249.2 4.8 %copy-start.7 = (f32[4,3,64,256]{3,2,1,0:T(8,128)S(1)}, f32[4,3,64,256]{3,2,1,0:T(8,128)}, u32[]{:S(2)}) copy-start(f32[4,3,64,256]{3,2,1,0:T(8,128)} %gather_fusion.3) | copy-start | bytes 2359300
  249.2 4.8 %copy-start.9 = (f32[4,3,64,256]{3,2,1,0:T(8,128)S(1)}, f32[4,3,64,256]{3,2,1,0:T(8,128)}, u32[]{:S(2)}) copy-start(f32[4,3,64,256]{3,2,1,0:T(8,128)} %gather_fusion.2) | copy-start | bytes 2359300
  249.2 4.8 %copy-start.11 = (f32[4,3,64,256]{3,2,1,0:T(8,128)S(1)}, f32[4,3,64,256]{3,2,1,0:T(8,128)}, u32[]{:S(2)}) copy-start(f32[4,3,64,256]{3,2,1,0:T(8,128)} %gather_fusion.1) | copy-start | bytes 2359300
  249.2 4.8 %copy-start.14 = (f32[3,1,4,64,128]{4,3,2,1,0:T(8,128)S(1)}, f32[3,1,4,64,128]{4,3,2,1,0:T(8,128)}, u32[]{:S(2)}) copy-start(f32[3,1,4,64,128]{4,3,2,1,0:T(8,128)} %param.10) | copy-start | bytes 1179652
  249.2 4.8 %copy-start.15 = (f32[4,64,256]{2,1,0:T(8,128)S(1)}, f32[4,64,256]{2,1,0:T(8,128)}, u32[]{:S(2)}) copy-start(f32[4,64,256]{2,1,0:T(8,128)} %get-tuple-element.40) | copy-start | bytes 786436
  261.7 1.1 copy-start.31
  293.8 44.9 %copy-start.35 = (s32[64]{0:T(128)S(1)}, s32[64]{0:T(128)}, u32[]{:S(2)}) copy-start(s32[64]{0:T(128)} %copy-done.34) | copy-start | bytes 772
  333.2 20.6 %all-to-all-start.1 = ((f32[64,3,1,4,1,128]{5,3,1,4,2,0:T(4,128)}), f32[64,3,1,4,1,128]{5,3,1,4,2,0:T(4,128)S(1)}, u32[]{:S(2)}, u32[]{:S(2)}) async-start(f32[64,3,1,4,1,128]{5,3,1,4,2,0:T(4,128)} %constant_dynamic-update-slice_fusion), calls=%async_computation.1 | async-start | bytes 786432 | tf_op jit(solution)/shard_map/all_to_all | solution.py:114
Sparse Core Ops, SparseCore 0:
  18.9 76.0 all-reduce.2
  98.4 150.7 all-reduce.4
